TPU v7x, 32 devices: a whole 2x2x4 slice. The times are simulated.
32 devices in a mesh: lon: 8 (over z, y), lat: 4 (over x, core).
Axes of the slice: x: 2, y: 2, z: 4, core: 2. Of those that a mesh axis runs over, the one named last changes fastest.
Arguments:
- sample_deviations: float32 [32, 32, 32, 1024], P(None, None, 'lat', 'lon'), may hold values from -6 to 6
- east_courant: float32 [32, 32, 1024], P(None, 'lat', 'lon'), may hold values from -0.45 to 0.45
- north_courant: float32 [32, 32, 1024], P(None, 'lat', 'lon'), may hold values from -0.45 to 0.45
- production: float32 [32, 32, 1024], P(None, 'lat', 'lon'), may hold values from -1.8 to 1.8
- loss_rate: float32 [32, 32, 1024], P(None, 'lat', 'lon'), may hold values from 0.02 to 0.3
- entry_count: int32 [32], P(('lon', 'lat')), may hold values from 24 to 48, as said below
- entry_row: int32 [1536], P(('lon', 'lat')), may hold values from 0 to 7
- entry_block: int32 [1536], P(('lon', 'lat')), may hold values from 0 to 15
- path_weight: bfloat16 [1536, 128, 128], P(('lon', 'lat')), may hold values from 0 to 0.15234375
- observed: float32 [16384], P(('lon', 'lat')), may hold values from -288 to 288
- obs_var: float32 [16384], P(('lon', 'lat')), may hold values from 64 to 4608, as said below
Outputs:
- updated_samples: float32 [32, 32, 32, 1024], P(None, None, 'lat', 'lon')
- prior_samples_in_path_space: float32 [32, 16384], P(None, ('lon', 'lat'))
- scaled_innovation: float32 [16384], P(('lon', 'lat'))
Inputs may be any that keep to these rules, and one draw needn't show every extreme that they name: `entry_count`: live crossing slots of each tile; some tile has all 48 live in every draw. `obs_var`: positive.
All inputs are finite; a program needn't handle non-finite values.
Results may differ from a plain program's by a relative error of at most 0.0025.
Values sent between devices are 32-bit elements; how exact they have to be, the bound alone decides.
No kernel may reach another device: no remote copies, remote signals or barrier semaphores. Data moves between devices by JAX's collectives and lax.ppermute only.
A program may use at most 64 MiB of HBM per device.

v0:
```python
import math
import jax
import jax.numpy as jnp
from jax import lax
from jax.sharding import PartitionSpec as P

ALTITUDE_LAYERS = 32
RAY_BLOCK = 128
BLOCKS_DEV = 4
SLOTS_TILE = 48
highest = lax.Precision.HIGHEST


def extended(x, sides, width, wrap):
    for axis, dim in sides:
        size, length = (lax.axis_size(axis), x.shape[dim])
        up = [(i, (i + 1) % size) for i in range(size if wrap else size - 1)]
        down = [(j, i) for i, j in up]
        last = lax.slice_in_dim(x, length - width, length, axis=dim)
        initial = lax.slice_in_dim(x, 0, width, axis=dim)
        before = lax.ppermute(last, axis, up)
        after = lax.ppermute(initial, axis, down)
        x = jnp.concatenate([before, x, after], axis=dim)
    return x


def advance(
    plasma_concentration,
    west_cell,
    east_cell,
    south_cell,
    north_cell,
    east_speed,
    north_speed,
    source,
    loss_rate,
):
    advected = (
        plasma_concentration
        - jnp.maximum(east_speed, 0.0) * (plasma_concentration - west_cell)
        - jnp.minimum(east_speed, 0.0) * (east_cell - plasma_concentration)
    )
    advected = (
        advected
        - jnp.maximum(north_speed, 0.0) * (plasma_concentration - south_cell)
        - jnp.minimum(north_speed, 0.0) * (north_cell - plasma_concentration)
    )
    return (1.0 - loss_rate) * advected + source


def analysis_weights(gram_sum, pull_sum):
    member_total = gram_sum.shape[0]
    identity = jnp.eye(member_total, dtype=gram_sum.dtype)
    factor_low = jnp.linalg.cholesky(gram_sum + (member_total - 1.0) * identity)
    halfway = lax.linalg.triangular_solve(factor_low, pull_sum[:, None], left_side=True, lower=True)
    mean_weights = lax.linalg.triangular_solve(
        factor_low, halfway, left_side=True, lower=True, transpose_a=True
    )
    inverse = lax.linalg.triangular_solve(factor_low, identity, left_side=True, lower=True)
    return mean_weights + math.sqrt(member_total - 1.0) * inverse.T


def ray_moments(ensemble, observed, obs_var):
    ray_mean = jnp.mean(ensemble, axis=0)
    spread = ensemble - ray_mean
    misfit = observed - ray_mean
    gram_sum = jnp.dot(spread / obs_var, spread.T, precision=highest)
    pull_sum = jnp.dot(spread, misfit / obs_var, precision=highest)
    return (gram_sum, pull_sum, misfit / jnp.sqrt(obs_var))


def per_device(
    sample_deviations,
    east_courant,
    north_courant,
    production,
    loss_rate,
    entry_count,
    entry_row,
    entry_block,
    path_weight,
    observed,
    obs_var,
):
    ensemble_size = sample_deviations.shape[0]
    plasma_concentration = sample_deviations
    for repeat in range(2):
        lon_framed = extended(plasma_concentration, (("lon", 3),), 1, True)
        lat_framed = extended(plasma_concentration, (("lat", 2),), 1, False)
        plasma_concentration = advance(
            plasma_concentration,
            lon_framed[..., :-2],
            lon_framed[..., 2:],
            lat_framed[..., :-2, :],
            lat_framed[..., 2:, :],
            east_courant,
            north_courant,
            production,
            loss_rate,
        )
    column_integral_total = (
        jnp.sum(plasma_concentration, axis=1) / math.sqrt(ALTITUDE_LAYERS)
    ).astype(jnp.bfloat16)
    picked = jnp.take(column_integral_total, entry_row, axis=1)
    partial_value = jnp.einsum(
        "mkc,kcr->kmr", picked, path_weight, preferred_element_type=jnp.float32
    )
    lat_size = lax.axis_size("lat")
    col_blocks = BLOCKS_DEV * lat_size
    live_slots = (jnp.arange(SLOTS_TILE) < entry_count[0]).astype(jnp.float32)
    slot_select = (entry_block[None, :] == jnp.arange(col_blocks)[:, None]).astype(
        jnp.float32
    ) * live_slots[None, :]
    summed = jnp.einsum("bk,kmr->mbr", slot_select, partial_value, precision=highest).reshape(
        ensemble_size, col_blocks * RAY_BLOCK
    )
    prior_samples_in_path_space = lax.psum_scatter(summed, "lat", scatter_dimension=1, tiled=True)
    gram_sum, pull_sum, scaled_innovation = ray_moments(
        prior_samples_in_path_space, observed, obs_var
    )
    gram_sum, pull_sum = lax.psum((gram_sum, pull_sum), ("lon", "lat"))
    transform = analysis_weights(gram_sum, pull_sum)
    raveled_grid_vector = plasma_concentration.reshape(ensemble_size, -1)
    centre = jnp.mean(raveled_grid_vector, axis=0)
    anomalies = raveled_grid_vector - centre
    updated_samples = centre + jnp.dot(transform.T, anomalies, precision=highest)
    return (
        updated_samples.reshape(plasma_concentration.shape),
        prior_samples_in_path_space,
        scaled_innovation,
    )


def solution(mesh):
    in_specs = (
        P(None, None, "lat", "lon"),
        P(None, "lat", "lon"),
        P(None, "lat", "lon"),
        P(None, "lat", "lon"),
        P(None, "lat", "lon"),
        P(("lon", "lat")),
        P(("lon", "lat")),
        P(("lon", "lat")),
        P(("lon", "lat"), None, None),
        P(("lon", "lat")),
        P(("lon", "lat")),
    )
    out_specs = (P(None, None, "lat", "lon"), P(None, ("lon", "lat")), P(("lon", "lat")))
    return jax.shard_map(
        per_device, mesh=mesh, in_specs=in_specs, out_specs=out_specs, check_vma=False
    )
```

profile of v0, /device:TPU:0, one launch (start us, length us, event | category | flops | bytes accessed | tf_op | source)
XLA Modules:
  0.0 201.4 jit_solution(16212824213112395093)
XLA Ops:
  7.2 8.1 %fusion.64 = (f32[32,32,8,1]{3,2,1,0:T(8,128)}, f32[32,32,8,1]{3,2,1,0:T(8,128)}) fusion(f32[32,32,8,128]{3,2,1,0:T(8,128)} %param.11), kind=kLoop, calls=%fused_computation.101 | loop fusion | bytes 131072 | tf_op jit(solution)/shard_map/slice | solution.py:19
  15.3 3.2 %copy.180 = f32[32,32,8,1]{1,2,3,0:T(8,128)S(1)} copy(f32[32,32,8,1]{3,2,1,0:T(8,128)} %get-tuple-element.12) | data formatting | bytes 65536
  18.6 3.0 %collective-permute-start = (f32[32,32,8,1]{1,2,3,0:T(8,128)S(1)}, f32[32,32,8,1]{1,2,3,0:T(8,128)}, u32[]{:S(2)}, u32[]{:S(2)}) collective-permute-start(f32[32,32,8,1]{1,2,3,0:T(8,128)S(1)} %copy.180), channel_id=1, source_target_pairs={{0,4},{4,8},{8,12},{12,16},{16,20},{20,24},{24,28},{28,0},{1,5},{5... | collective-permute-start | bytes 98312 | tf_op jit(solution)/shard_map/ppermute | solution.py:21
  21.6 3.8 %copy.181 = f32[32,32,8,1]{1,2,3,0:T(8,128)} copy(f32[32,32,8,1]{3,2,1,0:T(8,128)} %get-tuple-element.13) | data formatting | bytes 65536
  25.5 3.1 %collective-permute-start.1 = (f32[32,32,8,1]{1,2,3,0:T(8,128)}, f32[32,32,8,1]{1,2,3,0:T(8,128)}, u32[]{:S(2)}, u32[]{:S(2)}) collective-permute-start(f32[32,32,8,1]{1,2,3,0:T(8,128)} %copy.181), channel_id=1, source_target_pairs={{4,0},{8,4},{12,8},{16,12},{20,16},{24,20},{28,24},{0,28},{5,1},{9... | collective-permute-start | bytes 98312 | tf_op jit(solution)/shard_map/ppermute | solution.py:22
  28.6 5.4 %fusion.65 = (f32[32,32,1,128]{3,2,1,0:T(1,128)}, f32[32,32,1,128]{3,2,1,0:T(1,128)}) fusion(f32[32,32,8,128]{3,2,1,0:T(8,128)} %param.11), kind=kLoop, calls=%fused_computation.102 | loop fusion | bytes 2097152 | tf_op jit(solution)/shard_map/slice | solution.py:19
  38.5 3.8 %copy.159 = f32[32,32,8,1]{3,2,1,0:T(8,128)} copy(f32[32,32,8,1]{1,2,3,0:T(8,128)} %collective-permute-done) | data formatting | bytes 65536 | tf_op jit(solution)/shard_map/ppermute | solution.py:21
  42.3 3.8 %copy.161 = f32[32,32,8,1]{3,2,1,0:T(8,128)} copy(f32[32,32,8,1]{1,2,3,0:T(8,128)} %collective-permute-done.1) | data formatting | bytes 65536 | tf_op jit(solution)/shard_map/ppermute | solution.py:22
  46.2 12.7 %fusion.19 = f32[32,32,8,128]{3,2,1,0:T(8,128)S(1)} fusion(f32[32,32,8,128]{3,2,1,0:T(8,128)} %param.11, f32[32,32,1,128]{3,2,1,0:T(1,128)S(1)} %bitcast.69, f32[32,32,1,128]{3,2,1,0:T(1,128)S(1)} %bitcast.68, f32[32,32,8,1]{3,2,1,0:T(8,128)} %copy.161, f32[32,32,8,1]{3,2,1,0:T(8,128)} %copy.159, f32[32,8,128]{2,1,0:T(8,128)S(1)} %copy-done.2, ...), kind=kLoop, calls=%fused_computation.27 | loop fusion | flops 18874368 | bytes 10289152 | tf_op jit(solution)/shard_map/add | solution.py:48
  58.8 2.4 %fusion.63 = (f32[32,32,1,128]{3,2,1,0:T(1,128)}, f32[32,32,1,128]{3,2,1,0:T(1,128)}) fusion(f32[32,32,8,128]{3,2,1,0:T(8,128)S(1)} %fusion.19), kind=kLoop, calls=%fused_computation.100 | loop fusion | bytes 2097152 | tf_op jit(solution)/shard_map/slice | solution.py:19
  61.2 4.7 %collective-permute-start.6 = (f32[32,32,1,128]{3,1,2,0:T(8,128)}, f32[32,32,1,128]{3,1,2,0:T(8,128)S(1)}, u32[]{:S(2)}, u32[]{:S(2)}) collective-permute-start(f32[32,32,1,128]{3,1,2,0:T(8,128)} %bitcast.2), channel_id=1, source_target_pairs={{0,1},{1,2},{2,3},{4,5},{5,6},{6,7},{8,9},{9,10},{10,11},{12,13},{... | collective-permute-start | bytes 1572872 | tf_op jit(solution)/shard_map/ppermute | solution.py:21
  67.2 4.9 %fusion.62 = (f32[32,32,8,1]{3,2,1,0:T(8,128)}, f32[32,32,8,1]{3,2,1,0:T(8,128)}) fusion(f32[32,32,8,128]{3,2,1,0:T(8,128)S(1)} %fusion.19), kind=kLoop, calls=%fused_computation.99 | loop fusion | bytes 131072 | tf_op jit(solution)/shard_map/slice | solution.py:19
  72.1 3.2 %copy.166 = f32[32,32,8,1]{1,2,3,0:T(8,128)S(1)} copy(f32[32,32,8,1]{3,2,1,0:T(8,128)} %get-tuple-element.8) | data formatting | bytes 65536 | tf_op jit(solution)/shard_map/slice | solution.py:19
  75.4 3.8 %copy.168 = f32[32,32,8,1]{1,2,3,0:T(8,128)} copy(f32[32,32,8,1]{3,2,1,0:T(8,128)} %get-tuple-element.9) | data formatting | bytes 65536 | tf_op jit(solution)/shard_map/slice | solution.py:20
  79.2 4.7 %collective-permute-start.5 = (f32[32,32,8,1]{1,2,3,0:T(8,128)}, f32[32,32,8,1]{1,2,3,0:T(8,128)}, u32[]{:S(2)}, u32[]{:S(2)}) collective-permute-start(f32[32,32,8,1]{1,2,3,0:T(8,128)} %copy.168), channel_id=1, source_target_pairs={{4,0},{8,4},{12,8},{16,12},{20,16},{24,20},{28,24},{0,28},{5,1},{9... | collective-permute-start | bytes 98312 | tf_op jit(solution)/shard_map/ppermute | solution.py:22
  83.9 3.8 %copy.167 = f32[32,32,8,1]{3,2,1,0:T(8,128)} copy(f32[32,32,8,1]{1,2,3,0:T(8,128)} %collective-permute-done.4) | data formatting | bytes 65536 | tf_op jit(solution)/shard_map/ppermute | solution.py:21
  87.7 3.9 %copy.169 = f32[32,32,8,1]{3,2,1,0:T(8,128)} copy(f32[32,32,8,1]{1,2,3,0:T(8,128)} %collective-permute-done.5) | data formatting | bytes 65536 | tf_op jit(solution)/shard_map/ppermute | solution.py:22
  91.6 15.0 %fusion.60 = (f32[32,8,128]{2,1,0:T(8,128)S(1)}, f32[32,8,128]{2,1,0:T(8,128)S(1)}, f32[32,32,8,128]{3,2,1,0:T(8,128)}) fusion(f32[32,8,128]{2,1,0:T(8,128)S(1)} %copy-done.2, f32[32,32,8,128]{3,2,1,0:T(8,128)} %copy-done.1, f32[32,32,1,128]{3,2,1,0:T(1,128)S(1)} %bitcast.67, f32[32,8,128]{2,1,0:T(8,128)S(1)} %get-tuple-element.19, ...), kind=kLoop, calls=%fused_computation.98 | loop fusion | flops 20905984 | bytes 10551296 | tf_op jit(solution)/shard_map/reduce_sum | solution.py:124
  109.7 23.5 %reduce-scatter.2.cloned.1.call-done = f32[32,512]{1,0:T(8,128)} async-done(((f32[32,2048]{1,0:T(8,128)}), f32[32,512]{1,0:T(8,128)}) %reduce-scatter.2.cloned.1.call-update) | async-done | bytes 65552 | tf_op jit(solution)/shard_map/reduce_scatter | solution.py:117
  136.8 39.5 %all-reduce = (f32[32,32]{1,0:T(8,128)S(1)}, f32[32]{0:T(128)S(1)}) all-reduce(f32[32,32]{1,0:T(8,128)S(1)} %fusion.40, f32[32]{0:T(128)S(1)} %convolution_bitcast_fusion), channel_id=1, replica_groups=mesh['lon'=8,'lat'=4] {'lon','lat'}, use_global_device_ids=true, to_apply=%region_4.5 | all-reduce | flops 1056 | bytes 8448 | tf_op jit(solution)/shard_map/psum | solution.py:121
  176.3 2.9 %cholesky.17 = f32[32,32]{1,0:T(8,128)S(1)} custom-call(f32[32,32]{1,0:T(8,128)S(1)} %fusion.51), custom_call_target="Cholesky" | custom-call | tf_op jit(solution)/shard_map/jit(cholesky)/cholesky | solution.py:54
  180.6 2.4 %custom-call.10 = f32[1,32,32]{1,2,0:T(8,128)S(1)} custom-call(f32[1,32,32]{2,1,0:T(8,128)S(1)} %fusion.47), custom_call_target="InvertDiagBlocksLowerTriangular" | custom-call | tf_op jit(solution)/shard_map/triangular_solve | solution.py:56
  183.6 8.3 %fusion.29 = f32[4,8,256,128]{3,1,2,0:T(8,128)S(1)} fusion(f32[32,32]{1,0:T(8,128)S(1)} %fusion.31, f32[4,8,256,128]{3,2,1,0:T(8,128)} %bitcast.62, f32[32768]{0:T(1024)S(1)} %multiply_bitcast_fusion), kind=kOutput, calls=%fused_computation.40 | convolution fusion | flops 404750336 | bytes 8523776 | tf_op jit(solution)/shard_map/dot_general | solution.py:126
  191.8 2.8 %copy.186 = f32[4,8,256,128]{3,2,1,0:T(8,128)} copy(f32[4,8,256,128]{3,1,2,0:T(8,128)S(1)} %fusion.29) | data formatting | bytes 8388608
  (57 shorter events, 13.7 us)
Async XLA Ops:
  7.2 100.1 %copy-start = (bf16[48,128,128]{2,1,0:T(8,128)(2,1)S(1)}, bf16[48,128,128]{2,1,0:T(8,128)(2,1)}, u32[]{:S(2)}) copy-start(bf16[48,128,128]{2,1,0:T(8,128)(2,1)} %param.19) | copy-start | bytes 4718596
  7.2 126.0 %reduce-scatter.2.cloned.1.call-start = ((), (), s32[]{:S(2)}) async-start(), calls=%async_computation.1 | async-start | bytes 327680 | tf_op jit(solution)/shard_map/reduce_scatter | solution.py:117
  18.6 18.2 %copy-start.3 = (f32[32,8,128]{2,1,0:T(8,128)S(1)}, f32[32,8,128]{2,1,0:T(8,128)}, u32[]{:S(2)}) copy-start(f32[32,8,128]{2,1,0:T(8,128)} %param.15) | copy-start | bytes 393220
  18.6 18.2 %copy-start.8 = (s32[48]{0:T(128)S(1)}, s32[48]{0:T(128)}, u32[]{:S(2)}) copy-start(s32[48]{0:T(128)} %param.17) | copy-start | bytes 580
  18.6 18.3 %copy-start.4 = (f32[32,8,128]{2,1,0:T(8,128)S(1)}, f32[32,8,128]{2,1,0:T(8,128)}, u32[]{:S(2)}) copy-start(f32[32,8,128]{2,1,0:T(8,128)} %param.13) | copy-start | bytes 393220
  18.6 19.9 %collective-permute-start = (f32[32,32,8,1]{1,2,3,0:T(8,128)S(1)}, f32[32,32,8,1]{1,2,3,0:T(8,128)}, u32[]{:S(2)}, u32[]{:S(2)}) collective-permute-start(f32[32,32,8,1]{1,2,3,0:T(8,128)S(1)} %copy.180), channel_id=1, source_target_pairs={{0,4},{4,8},{8,12},{12,16},{16,20},{20,24},{24,28},{28,0},{1,5},{5... | collective-permute-start | bytes 98312 | tf_op jit(solution)/shard_map/ppermute | solution.py:21
  25.5 16.8 %collective-permute-start.1 = (f32[32,32,8,1]{1,2,3,0:T(8,128)}, f32[32,32,8,1]{1,2,3,0:T(8,128)}, u32[]{:S(2)}, u32[]{:S(2)}) collective-permute-start(f32[32,32,8,1]{1,2,3,0:T(8,128)} %copy.181), channel_id=1, source_target_pairs={{4,0},{8,4},{12,8},{16,12},{20,16},{24,20},{28,24},{0,28},{5,1},{9... | collective-permute-start | bytes 98312 | tf_op jit(solution)/shard_map/ppermute | solution.py:22
  34.0 12.1 %collective-permute-start.2 = (f32[32,32,1,128]{3,1,2,0:T(8,128)}, f32[32,32,1,128]{3,1,2,0:T(8,128)S(1)}, u32[]{:S(2)}, u32[]{:S(2)}) collective-permute-start(f32[32,32,1,128]{3,1,2,0:T(8,128)} %bitcast.20), channel_id=1, source_target_pairs={{0,1},{1,2},{2,3},{4,5},{5,6},{6,7},{8,9},{9,10},{10,11},{12,13},{... | collective-permute-start | bytes 1572872 | tf_op jit(solution)/shard_map/ppermute | solution.py:21
  35.5 10.7 %collective-permute-start.3 = (f32[32,32,1,128]{3,1,2,0:T(8,128)}, f32[32,32,1,128]{3,1,2,0:T(8,128)S(1)}, u32[]{:S(2)}, u32[]{:S(2)}) collective-permute-start(f32[32,32,1,128]{3,1,2,0:T(8,128)} %bitcast.21), channel_id=1, source_target_pairs={{1,0},{2,1},{3,2},{5,4},{6,5},{7,6},{9,8},{10,9},{11,10},{13,12},{... | collective-permute-start | bytes 1572872 | tf_op jit(solution)/shard_map/ppermute | solution.py:22
  38.5 7.7 %copy-start.2 = (f32[32,8,128]{2,1,0:T(8,128)S(1)}, f32[32,8,128]{2,1,0:T(8,128)}, u32[]{:S(2)}) copy-start(f32[32,8,128]{2,1,0:T(8,128)} %param.14) | copy-start | bytes 393220
  58.8 13.3 %copy-start.1 = (f32[32,32,8,128]{3,2,1,0:T(8,128)}, f32[32,32,8,128]{3,2,1,0:T(8,128)S(1)}, u32[]{:S(2)}) copy-start(f32[32,32,8,128]{3,2,1,0:T(8,128)S(1)} %fusion.19) | copy-start | bytes 12582916
  61.2 30.4 %collective-permute-start.6 = (f32[32,32,1,128]{3,1,2,0:T(8,128)}, f32[32,32,1,128]{3,1,2,0:T(8,128)S(1)}, u32[]{:S(2)}, u32[]{:S(2)}) collective-permute-start(f32[32,32,1,128]{3,1,2,0:T(8,128)} %bitcast.2), channel_id=1, source_target_pairs={{0,1},{1,2},{2,3},{4,5},{5,6},{6,7},{8,9},{9,10},{10,11},{12,13},{... | collective-permute-start | bytes 1572872 | tf_op jit(solution)/shard_map/ppermute | solution.py:21
  65.9 25.7 %collective-permute-start.7 = (f32[32,32,1,128]{3,1,2,0:T(8,128)}, f32[32,32,1,128]{3,1,2,0:T(8,128)S(1)}, u32[]{:S(2)}, u32[]{:S(2)}) collective-permute-start(f32[32,32,1,128]{3,1,2,0:T(8,128)} %bitcast.4), channel_id=1, source_target_pairs={{1,0},{2,1},{3,2},{5,4},{6,5},{7,6},{9,8},{10,9},{11,10},{13,12},{... | collective-permute-start | bytes 1572872 | tf_op jit(solution)/shard_map/ppermute | solution.py:22
  75.3 8.6 %collective-permute-start.4 = (f32[32,32,8,1]{1,2,3,0:T(8,128)S(1)}, f32[32,32,8,1]{1,2,3,0:T(8,128)}, u32[]{:S(2)}, u32[]{:S(2)}) collective-permute-start(f32[32,32,8,1]{1,2,3,0:T(8,128)S(1)} %copy.166), channel_id=1, source_target_pairs={{0,4},{4,8},{8,12},{12,16},{16,20},{20,24},{24,28},{28,0},{1,5},{5... | collective-permute-start | bytes 98312 | tf_op jit(solution)/shard_map/ppermute | solution.py:21
  79.2 8.5 %collective-permute-start.5 = (f32[32,32,8,1]{1,2,3,0:T(8,128)}, f32[32,32,8,1]{1,2,3,0:T(8,128)}, u32[]{:S(2)}, u32[]{:S(2)}) collective-permute-start(f32[32,32,8,1]{1,2,3,0:T(8,128)} %copy.168), channel_id=1, source_target_pairs={{4,0},{8,4},{12,8},{16,12},{20,16},{24,20},{28,24},{0,28},{5,1},{9... | collective-permute-start | bytes 98312 | tf_op jit(solution)/shard_map/ppermute | solution.py:22
  91.6 16.3 %copy-start.7 = (s32[48]{0:T(128)S(1)}, s32[48]{0:T(128)}, u32[]{:S(2)}) copy-start(s32[48]{0:T(128)} %param.18) | copy-start | bytes 580
  106.6 27.5 %copy-start.5 = (f32[512]{0:T(512)S(1)}, f32[512]{0:T(512)}, u32[]{:S(2)}) copy-start(f32[512]{0:T(512)} %param.20) | copy-start | bytes 6148
  106.6 27.5 %copy-start.6 = (f32[512]{0:T(512)S(1)}, f32[512]{0:T(512)}, u32[]{:S(2)}) copy-start(f32[512]{0:T(512)} %param.21) | copy-start | bytes 6148
Sparse Core Ops, SparseCore 0:
  109.8 23.3 reduce-scatter.1
where the time goes:
time: 202 us; the launch traced here: 201 us
  local copies, waits for them, and re-layouts  54.5 us (27%)
  blocking collectives  39.5 us (20%)
  other arithmetic  36.8 us (18%)
  waiting for transfers between devices  23.6 us (12%)
  starting transfers between devices  19.7 us (10%)
  between operations  14.9 us (7%)
  matrix products  12.5 us (6%)
    psum x1, blocking collectives, per_device(): gram_sum, pull_sum = lax.psum((gram_sum, pull_sum), ('lon', 'lat'))  39.5 us
    slice x5, local copies, waits for them, and re-layouts, extended(): last = lax.slice_in_dim(x, length - width, length, axis=dim)  24 us
    reduce_scatter x1, waiting for transfers between devices, per_device(): lax.psum_scatter(summed, 'lat', scatter_dimension=1, tiled=True)  23.5 us
    reduce_sum x1, other arithmetic, per_device(): centre = jnp.mean(raveled_grid_vector, axis=0)  15 us
    add x1, other arithmetic, advance(): return (1.0 - loss_rate) * advected + source  12.7 us
    unnamed x22, local copies, waits for them, and re-layouts  10.7 us
    ppermute x4, starting transfers between devices, extended(): after = lax.ppermute(initial, axis, down)  10.4 us
    ppermute x4, starting transfers between devices, extended(): before = lax.ppermute(last, axis, up)  9.26 us
  transfers between devices with their start and end apart: 9, of which 1 were waited for; matrix products, arithmetic and copies ran while one was open for 19% of the time, Pallas kernels for 0%

commit v1 on v0

--- a/solution.py
+++ b/solution.py
@@ -118,7 +118,7 @@
     gram_sum, pull_sum, scaled_innovation = ray_moments(
         prior_samples_in_path_space, observed, obs_var
     )
-    gram_sum, pull_sum = lax.psum((gram_sum, pull_sum), ("lon", "lat"))
+    gram_sum, pull_sum = lax.psum(lax.psum((gram_sum, pull_sum), "lat"), "lon")
     transform = analysis_weights(gram_sum, pull_sum)
     raveled_grid_vector = plasma_concentration.reshape(ensemble_size, -1)
     centre = jnp.mean(raveled_grid_vector, axis=0)

time: 202 us -> 210 us (1.040)
  blocking collectives: 39.5 us -> 47.4 us
    psum x1 -> x2, blocking collectives: 39.5 us -> 47.4 us  [per_device(): gram_sum, pull_sum = lax.psum(lax.psum((gram_sum, pull_sum), 'lat'), 'lon')]
  transfers between devices with their start and end apart: 9 -> 9, of which waited for: 1 -> 1; matrix products, arithmetic and copies ran while one was open for 19% -> 18% of each run, Pallas kernels for 0% -> 0%
where the time goes in v1:
time: 210 us; the launch traced here: 209 us
  local copies, waits for them, and re-layouts  54.5 us (26%)
  blocking collectives  47.4 us (23%)
  other arithmetic  36.8 us (18%)
  waiting for transfers between devices  23.6 us (11%)
  starting transfers between devices  19.7 us (9%)
  between operations  14.9 us (7%)
  matrix products  12.5 us (6%)
    psum x2, blocking collectives, per_device(): gram_sum, pull_sum = lax.psum(lax.psum((gram_sum, pull_sum), 'lat'), 'lon')  47.4 us
    slice x5, local copies, waits for them, and re-layouts, extended(): last = lax.slice_in_dim(x, length - width, length, axis=dim)  24 us
    reduce_scatter x1, waiting for transfers between devices, per_device(): lax.psum_scatter(summed, 'lat', scatter_dimension=1, tiled=True)  23.5 us
    reduce_sum x1, other arithmetic, per_device(): centre = jnp.mean(raveled_grid_vector, axis=0)  15 us
    add x1, other arithmetic, advance(): return (1.0 - loss_rate) * advected + source  12.7 us
    unnamed x22, local copies, waits for them, and re-layouts  10.7 us
    ppermute x4, starting transfers between devices, extended(): after = lax.ppermute(initial, axis, down)  10.4 us
    ppermute x4, starting transfers between devices, extended(): before = lax.ppermute(last, axis, up)  9.26 us
  transfers between devices with their start and end apart: 9, of which 1 were waited for; matrix products, arithmetic and copies ran while one was open for 18% of the time, Pallas kernels for 0%

profile of v1, /device:TPU:0, one launch (start us, length us, event | category | flops | bytes accessed | tf_op | source)
XLA Modules:
  0.0 209.4 jit_solution(13729498884485307832)
XLA Ops:
  7.2 8.1 %fusion.64 = (f32[32,32,8,1]{3,2,1,0:T(8,128)}, f32[32,32,8,1]{3,2,1,0:T(8,128)}) fusion(f32[32,32,8,128]{3,2,1,0:T(8,128)} %param.11), kind=kLoop, calls=%fused_computation.101 | loop fusion | bytes 131072 | tf_op jit(solution)/shard_map/slice | solution.py:19
  15.3 3.2 %copy.180 = f32[32,32,8,1]{1,2,3,0:T(8,128)S(1)} copy(f32[32,32,8,1]{3,2,1,0:T(8,128)} %get-tuple-element.14) | data formatting | bytes 65536
  18.6 3.0 %collective-permute-start = (f32[32,32,8,1]{1,2,3,0:T(8,128)S(1)}, f32[32,32,8,1]{1,2,3,0:T(8,128)}, u32[]{:S(2)}, u32[]{:S(2)}) collective-permute-start(f32[32,32,8,1]{1,2,3,0:T(8,128)S(1)} %copy.180), channel_id=1, source_target_pairs={{0,4},{4,8},{8,12},{12,16},{16,20},{20,24},{24,28},{28,0},{1,5},{5... | collective-permute-start | bytes 98312 | tf_op jit(solution)/shard_map/ppermute | solution.py:21
  21.6 3.8 %copy.181 = f32[32,32,8,1]{1,2,3,0:T(8,128)} copy(f32[32,32,8,1]{3,2,1,0:T(8,128)} %get-tuple-element.15) | data formatting | bytes 65536
  25.5 3.1 %collective-permute-start.1 = (f32[32,32,8,1]{1,2,3,0:T(8,128)}, f32[32,32,8,1]{1,2,3,0:T(8,128)}, u32[]{:S(2)}, u32[]{:S(2)}) collective-permute-start(f32[32,32,8,1]{1,2,3,0:T(8,128)} %copy.181), channel_id=1, source_target_pairs={{4,0},{8,4},{12,8},{16,12},{20,16},{24,20},{28,24},{0,28},{5,1},{9... | collective-permute-start | bytes 98312 | tf_op jit(solution)/shard_map/ppermute | solution.py:22
  28.6 5.4 %fusion.65 = (f32[32,32,1,128]{3,2,1,0:T(1,128)}, f32[32,32,1,128]{3,2,1,0:T(1,128)}) fusion(f32[32,32,8,128]{3,2,1,0:T(8,128)} %param.11), kind=kLoop, calls=%fused_computation.102 | loop fusion | bytes 2097152 | tf_op jit(solution)/shard_map/slice | solution.py:19
  38.5 3.8 %copy.159 = f32[32,32,8,1]{3,2,1,0:T(8,128)} copy(f32[32,32,8,1]{1,2,3,0:T(8,128)} %collective-permute-done) | data formatting | bytes 65536 | tf_op jit(solution)/shard_map/ppermute | solution.py:21
  42.3 3.8 %copy.161 = f32[32,32,8,1]{3,2,1,0:T(8,128)} copy(f32[32,32,8,1]{1,2,3,0:T(8,128)} %collective-permute-done.1) | data formatting | bytes 65536 | tf_op jit(solution)/shard_map/ppermute | solution.py:22
  46.1 12.7 %fusion.19 = f32[32,32,8,128]{3,2,1,0:T(8,128)S(1)} fusion(f32[32,32,8,128]{3,2,1,0:T(8,128)} %param.11, f32[32,32,1,128]{3,2,1,0:T(1,128)S(1)} %bitcast.69, f32[32,32,1,128]{3,2,1,0:T(1,128)S(1)} %bitcast.68, f32[32,32,8,1]{3,2,1,0:T(8,128)} %copy.161, f32[32,32,8,1]{3,2,1,0:T(8,128)} %copy.159, f32[32,8,128]{2,1,0:T(8,128)S(1)} %copy-done.2, ...), kind=kLoop, calls=%fused_computation.27 | loop fusion | flops 18874368 | bytes 10289152 | tf_op jit(solution)/shard_map/add | solution.py:48
  61.2 4.7 %collective-permute-start.6 = (f32[32,32,1,128]{3,1,2,0:T(8,128)}, f32[32,32,1,128]{3,1,2,0:T(8,128)S(1)}, u32[]{:S(2)}, u32[]{:S(2)}) collective-permute-start(f32[32,32,1,128]{3,1,2,0:T(8,128)} %bitcast.2), channel_id=1, source_target_pairs={{0,1},{1,2},{2,3},{4,5},{5,6},{6,7},{8,9},{9,10},{10,11},{12,13},{... | collective-permute-start | bytes 1572872 | tf_op jit(solution)/shard_map/ppermute | solution.py:21
  67.2 4.9 %fusion.62 = (f32[32,32,8,1]{3,2,1,0:T(8,128)}, f32[32,32,8,1]{3,2,1,0:T(8,128)}) fusion(f32[32,32,8,128]{3,2,1,0:T(8,128)S(1)} %fusion.19), kind=kLoop, calls=%fused_computation.99 | loop fusion | bytes 131072 | tf_op jit(solution)/shard_map/slice | solution.py:19
  72.1 3.2 %copy.166 = f32[32,32,8,1]{1,2,3,0:T(8,128)S(1)} copy(f32[32,32,8,1]{3,2,1,0:T(8,128)} %get-tuple-element.10) | data formatting | bytes 65536 | tf_op jit(solution)/shard_map/slice | solution.py:19
  75.3 3.8 %copy.168 = f32[32,32,8,1]{1,2,3,0:T(8,128)} copy(f32[32,32,8,1]{3,2,1,0:T(8,128)} %get-tuple-element.11) | data formatting | bytes 65536 | tf_op jit(solution)/shard_map/slice | solution.py:20
  79.2 4.7 %collective-permute-start.5 = (f32[32,32,8,1]{1,2,3,0:T(8,128)}, f32[32,32,8,1]{1,2,3,0:T(8,128)}, u32[]{:S(2)}, u32[]{:S(2)}) collective-permute-start(f32[32,32,8,1]{1,2,3,0:T(8,128)} %copy.168), channel_id=1, source_target_pairs={{4,0},{8,4},{12,8},{16,12},{20,16},{24,20},{28,24},{0,28},{5,1},{9... | collective-permute-start | bytes 98312 | tf_op jit(solution)/shard_map/ppermute | solution.py:22
  83.9 3.8 %copy.167 = f32[32,32,8,1]{3,2,1,0:T(8,128)} copy(f32[32,32,8,1]{1,2,3,0:T(8,128)} %collective-permute-done.4) | data formatting | bytes 65536 | tf_op jit(solution)/shard_map/ppermute | solution.py:21
  87.7 3.8 %copy.169 = f32[32,32,8,1]{3,2,1,0:T(8,128)} copy(f32[32,32,8,1]{1,2,3,0:T(8,128)} %collective-permute-done.5) | data formatting | bytes 65536 | tf_op jit(solution)/shard_map/ppermute | solution.py:22
  91.5 15.0 %fusion.60 = (f32[32,8,128]{2,1,0:T(8,128)S(1)}, f32[32,8,128]{2,1,0:T(8,128)S(1)}, f32[32,32,8,128]{3,2,1,0:T(8,128)}) fusion(f32[32,8,128]{2,1,0:T(8,128)S(1)} %copy-done.2, f32[32,32,8,128]{3,2,1,0:T(8,128)} %copy-done.1, f32[32,32,1,128]{3,2,1,0:T(1,128)S(1)} %bitcast.67, f32[32,8,128]{2,1,0:T(8,128)S(1)} %get-tuple-element.21, ...), kind=kLoop, calls=%fused_computation.98 | loop fusion | flops 20905984 | bytes 10551296 | tf_op jit(solution)/shard_map/reduce_sum | solution.py:124
  109.6 23.5 %reduce-scatter.2.cloned.1.call-done = f32[32,512]{1,0:T(8,128)} async-done(((f32[32,2048]{1,0:T(8,128)}), f32[32,512]{1,0:T(8,128)}) %reduce-scatter.2.cloned.1.call-update) | async-done | bytes 65552 | tf_op jit(solution)/shard_map/reduce_scatter | solution.py:117
  136.7 10.3 %all-reduce.1 = (f32[32,32]{1,0:T(8,128)S(1)}, f32[32]{0:T(128)S(1)}) all-reduce(f32[32,32]{1,0:T(8,128)S(1)} %fusion.40, f32[32]{0:T(128)S(1)} %convolution_bitcast_fusion), channel_id=1, replica_groups=mesh['lon'=8,'lat'=4] {'lat'}, use_global_device_ids=true, to_apply=%region_4.5 | all-reduce | flops 1056 | bytes 8448 | tf_op jit(solution)/shard_map/psum | solution.py:121
  147.0 37.2 %all-reduce = (f32[32,32]{1,0:T(8,128)S(1)}, f32[32]{0:T(128)S(1)}) all-reduce(f32[32,32]{1,0:T(8,128)S(1)} %get-tuple-element.7, f32[32]{0:T(128)S(1)} %get-tuple-element.8), channel_id=1, replica_groups=mesh['lon'=8,'lat'=4] {'lon'}, use_global_device_ids=true, to_apply=%region_5.6 | all-reduce | flops 1056 | bytes 8448 | tf_op jit(solution)/shard_map/psum | solution.py:121
  184.3 2.9 %cholesky.17 = f32[32,32]{1,0:T(8,128)S(1)} custom-call(f32[32,32]{1,0:T(8,128)S(1)} %fusion.51), custom_call_target="Cholesky" | custom-call | tf_op jit(solution)/shard_map/jit(cholesky)/cholesky | solution.py:54
  188.5 2.4 %custom-call.10 = f32[1,32,32]{1,2,0:T(8,128)S(1)} custom-call(f32[1,32,32]{2,1,0:T(8,128)S(1)} %fusion.47), custom_call_target="InvertDiagBlocksLowerTriangular" | custom-call | tf_op jit(solution)/shard_map/triangular_solve | solution.py:56
  191.5 8.3 %fusion.29 = f32[4,8,256,128]{3,1,2,0:T(8,128)S(1)} fusion(f32[32,32]{1,0:T(8,128)S(1)} %fusion.31, f32[4,8,256,128]{3,2,1,0:T(8,128)} %bitcast.62, f32[32768]{0:T(1024)S(1)} %multiply_bitcast_fusion), kind=kOutput, calls=%fused_computation.40 | convolution fusion | flops 404750336 | bytes 8523776 | tf_op jit(solution)/shard_map/dot_general | solution.py:126
  199.8 2.8 %copy.186 = f32[4,8,256,128]{3,2,1,0:T(8,128)} copy(f32[4,8,256,128]{3,1,2,0:T(8,128)S(1)} %fusion.29) | data formatting | bytes 8388608
  (58 shorter events, 16.1 us)
Async XLA Ops:
  7.2 100.1 %copy-start = (bf16[48,128,128]{2,1,0:T(8,128)(2,1)S(1)}, bf16[48,128,128]{2,1,0:T(8,128)(2,1)}, u32[]{:S(2)}) copy-start(bf16[48,128,128]{2,1,0:T(8,128)(2,1)} %param.19) | copy-start | bytes 4718596
  7.2 126.0 %reduce-scatter.2.cloned.1.call-start = ((), (), s32[]{:S(2)}) async-start(), calls=%async_computation.1 | async-start | bytes 327680 | tf_op jit(solution)/shard_map/reduce_scatter | solution.py:117
  18.6 18.2 %copy-start.3 = (f32[32,8,128]{2,1,0:T(8,128)S(1)}, f32[32,8,128]{2,1,0:T(8,128)}, u32[]{:S(2)}) copy-start(f32[32,8,128]{2,1,0:T(8,128)} %param.15) | copy-start | bytes 393220
  18.6 18.2 %copy-start.8 = (s32[48]{0:T(128)S(1)}, s32[48]{0:T(128)}, u32[]{:S(2)}) copy-start(s32[48]{0:T(128)} %param.17) | copy-start | bytes 580
  18.6 18.3 %copy-start.4 = (f32[32,8,128]{2,1,0:T(8,128)S(1)}, f32[32,8,128]{2,1,0:T(8,128)}, u32[]{:S(2)}) copy-start(f32[32,8,128]{2,1,0:T(8,128)} %param.13) | copy-start | bytes 393220
  18.6 19.9 %collective-permute-start = (f32[32,32,8,1]{1,2,3,0:T(8,128)S(1)}, f32[32,32,8,1]{1,2,3,0:T(8,128)}, u32[]{:S(2)}, u32[]{:S(2)}) collective-permute-start(f32[32,32,8,1]{1,2,3,0:T(8,128)S(1)} %copy.180), channel_id=1, source_target_pairs={{0,4},{4,8},{8,12},{12,16},{16,20},{20,24},{24,28},{28,0},{1,5},{5... | collective-permute-start | bytes 98312 | tf_op jit(solution)/shard_map/ppermute | solution.py:21
  25.5 16.8 %collective-permute-start.1 = (f32[32,32,8,1]{1,2,3,0:T(8,128)}, f32[32,32,8,1]{1,2,3,0:T(8,128)}, u32[]{:S(2)}, u32[]{:S(2)}) collective-permute-start(f32[32,32,8,1]{1,2,3,0:T(8,128)} %copy.181), channel_id=1, source_target_pairs={{4,0},{8,4},{12,8},{16,12},{20,16},{24,20},{28,24},{0,28},{5,1},{9... | collective-permute-start | bytes 98312 | tf_op jit(solution)/shard_map/ppermute | solution.py:22
  34.0 12.1 %collective-permute-start.2 = (f32[32,32,1,128]{3,1,2,0:T(8,128)}, f32[32,32,1,128]{3,1,2,0:T(8,128)S(1)}, u32[]{:S(2)}, u32[]{:S(2)}) collective-permute-start(f32[32,32,1,128]{3,1,2,0:T(8,128)} %bitcast.20), channel_id=1, source_target_pairs={{0,1},{1,2},{2,3},{4,5},{5,6},{6,7},{8,9},{9,10},{10,11},{12,13},{... | collective-permute-start | bytes 1572872 | tf_op jit(solution)/shard_map/ppermute | solution.py:21
  35.5 10.7 %collective-permute-start.3 = (f32[32,32,1,128]{3,1,2,0:T(8,128)}, f32[32,32,1,128]{3,1,2,0:T(8,128)S(1)}, u32[]{:S(2)}, u32[]{:S(2)}) collective-permute-start(f32[32,32,1,128]{3,1,2,0:T(8,128)} %bitcast.21), channel_id=1, source_target_pairs={{1,0},{2,1},{3,2},{5,4},{6,5},{7,6},{9,8},{10,9},{11,10},{13,12},{... | collective-permute-start | bytes 1572872 | tf_op jit(solution)/shard_map/ppermute | solution.py:22
  38.5 7.7 %copy-start.2 = (f32[32,8,128]{2,1,0:T(8,128)S(1)}, f32[32,8,128]{2,1,0:T(8,128)}, u32[]{:S(2)}) copy-start(f32[32,8,128]{2,1,0:T(8,128)} %param.14) | copy-start | bytes 393220
  58.8 13.2 %copy-start.1 = (f32[32,32,8,128]{3,2,1,0:T(8,128)}, f32[32,32,8,128]{3,2,1,0:T(8,128)S(1)}, u32[]{:S(2)}) copy-start(f32[32,32,8,128]{3,2,1,0:T(8,128)S(1)} %fusion.19) | copy-start | bytes 12582916
  61.2 30.4 %collective-permute-start.6 = (f32[32,32,1,128]{3,1,2,0:T(8,128)}, f32[32,32,1,128]{3,1,2,0:T(8,128)S(1)}, u32[]{:S(2)}, u32[]{:S(2)}) collective-permute-start(f32[32,32,1,128]{3,1,2,0:T(8,128)} %bitcast.2), channel_id=1, source_target_pairs={{0,1},{1,2},{2,3},{4,5},{5,6},{6,7},{8,9},{9,10},{10,11},{12,13},{... | collective-permute-start | bytes 1572872 | tf_op jit(solution)/shard_map/ppermute | solution.py:21
  65.9 25.7 %collective-permute-start.7 = (f32[32,32,1,128]{3,1,2,0:T(8,128)}, f32[32,32,1,128]{3,1,2,0:T(8,128)S(1)}, u32[]{:S(2)}, u32[]{:S(2)}) collective-permute-start(f32[32,32,1,128]{3,1,2,0:T(8,128)} %bitcast.4), channel_id=1, source_target_pairs={{1,0},{2,1},{3,2},{5,4},{6,5},{7,6},{9,8},{10,9},{11,10},{13,12},{... | collective-permute-start | bytes 1572872 | tf_op jit(solution)/shard_map/ppermute | solution.py:22
  75.3 8.6 %collective-permute-start.4 = (f32[32,32,8,1]{1,2,3,0:T(8,128)S(1)}, f32[32,32,8,1]{1,2,3,0:T(8,128)}, u32[]{:S(2)}, u32[]{:S(2)}) collective-permute-start(f32[32,32,8,1]{1,2,3,0:T(8,128)S(1)} %copy.166), channel_id=1, source_target_pairs={{0,4},{4,8},{8,12},{12,16},{16,20},{20,24},{24,28},{28,0},{1,5},{5... | collective-permute-start | bytes 98312 | tf_op jit(solution)/shard_map/ppermute | solution.py:21
  79.2 8.5 %collective-permute-start.5 = (f32[32,32,8,1]{1,2,3,0:T(8,128)}, f32[32,32,8,1]{1,2,3,0:T(8,128)}, u32[]{:S(2)}, u32[]{:S(2)}) collective-permute-start(f32[32,32,8,1]{1,2,3,0:T(8,128)} %copy.168), channel_id=1, source_target_pairs={{4,0},{8,4},{12,8},{16,12},{20,16},{24,20},{28,24},{0,28},{5,1},{9... | collective-permute-start | bytes 98312 | tf_op jit(solution)/shard_map/ppermute | solution.py:22
  91.5 16.3 %copy-start.7 = (s32[48]{0:T(128)S(1)}, s32[48]{0:T(128)}, u32[]{:S(2)}) copy-start(s32[48]{0:T(128)} %param.18) | copy-start | bytes 580
  106.5 27.5 %copy-start.5 = (f32[512]{0:T(512)S(1)}, f32[512]{0:T(512)}, u32[]{:S(2)}) copy-start(f32[512]{0:T(512)} %param.20) | copy-start | bytes 6148
  106.5 27.5 %copy-start.6 = (f32[512]{0:T(512)S(1)}, f32[512]{0:T(512)}, u32[]{:S(2)}) copy-start(f32[512]{0:T(512)} %param.21) | copy-start | bytes 6148
Sparse Core Ops, SparseCore 0:
  109.7 23.3 reduce-scatter.1
